TPU v7x, 128 devices: a whole 4x4x4 slice. The times are simulated.
128 devices in a mesh: seq: 32 (over y, x, core), tp: 4 (over z).
Axes of the slice: x: 4, y: 4, z: 4, core: 2. Of those that a mesh axis runs over, the one named last changes fastest.
Arguments:
- codes: bfloat16 [16384, 4096], P('seq', 'tp'), may hold values from -127 to 127, as said below
- exponents: int32 [16384], P('seq'), may hold values from -8 to -5
- w_query: bfloat16 [4096, 4096], P(None, 'tp'), may hold values from -0.09375 to 0.09375
- w_key: bfloat16 [4096, 4096], P(None, 'tp'), may hold values from -0.09375 to 0.09375
- w_value: bfloat16 [4096, 4096], P(None, 'tp'), may hold values from -0.09375 to 0.09375
- norm_gain: float32 [4096], P('tp'), may hold values from 0.1 to 1.9
- w_out: bfloat16 [4096, 4096], P('tp'), may hold values from -0.09375 to 0.09375
Outputs:
- mixed: bfloat16 [16384, 4096], P(('seq', 'tp'))
Inputs may be any that keep to these rules, and one draw needn't show every extreme that they name: `codes`: every entry is a whole number.
All inputs are finite; a program needn't handle non-finite values.
Results may differ from a plain program's by a relative error of at most 0.012.
Values may be sent and summed in bfloat16 or wider, within the bound.
No kernel may reach another device: no remote copies, remote signals or barrier semaphores. Data moves between devices by JAX's collectives and lax.ppermute only.
A program may use at most 128 MiB of HBM per device.

v0:
```python
import jax
import jax.numpy as jnp
from jax import lax
from jax.sharding import PartitionSpec as P

HD = 128
BLK = 512


def prefix(x, axis, combine, identity):
    length, place = (lax.axis_size(axis), lax.axis_index(axis))
    everything = lax.all_gather(x, axis)
    start = jnp.broadcast_to(jnp.asarray(identity, x.dtype), x.shape)

    def step(k, before):
        reached = k < place
        new = combine(before, everything[k])
        return jnp.where(reached, new, before)

    return lax.fori_loop(0, length, step, start)


def on_device(codes, exponents, w_query, w_key, w_value, norm_gain, w_out):
    tok_count = codes.shape[0]
    local_width = w_query.shape[1]
    heads_local = local_width // HD
    blocks = tok_count // BLK
    row_scale = jnp.exp2(exponents.astype(jnp.float32))[:, None]
    weights = (w_query, w_key, w_value)
    piece = lax.all_gather(codes, "tp", axis=1, tiled=True)
    query, keys, values = tuple(
        (jnp.dot(piece, weight, preferred_element_type=jnp.float32) for weight in weights)
    )
    feat_q = (
        (jax.nn.elu(query * row_scale) + 1.0)
        .astype(jnp.bfloat16)
        .reshape(blocks, BLK, heads_local, HD)
    )
    feat_k = (
        (jax.nn.elu(keys * row_scale) + 1.0)
        .astype(jnp.bfloat16)
        .reshape(blocks, BLK, heads_local, HD)
    )
    value_b = (values * row_scale).astype(jnp.bfloat16).reshape(blocks, BLK, heads_local, HD)
    block_states = jnp.einsum(
        "bshd,bshe->bhde", feat_k, value_b, preferred_element_type=jnp.float32
    )
    shard_state = jnp.sum(block_states, axis=0)
    zero_state = jnp.zeros((heads_local, HD, HD), jnp.float32)
    before = prefix(shard_state, "seq", lambda earlier, later: earlier + later, zero_state)
    states = (before[None] + (jnp.cumsum(block_states, axis=0) - block_states)).astype(jnp.bfloat16)
    inter = jnp.einsum("bshd,bhde->bshe", feat_q, states, preferred_element_type=jnp.float32)
    causal = jnp.tril(jnp.ones((BLK, BLK), jnp.float32))
    scores = jnp.einsum("bshd,bthd->bhst", feat_q, feat_k, preferred_element_type=jnp.float32)
    scores = (scores * causal[None, None]).astype(jnp.bfloat16)
    intra = jnp.einsum("bhst,bthe->bshe", scores, value_b, preferred_element_type=jnp.float32)
    summed = inter + intra
    mean_sq = jnp.mean(summed * summed, axis=-1, keepdims=True)
    gain = norm_gain.reshape(heads_local, HD)
    normed = (
        (summed * lax.rsqrt(mean_sq + 1e-05) * gain)
        .astype(jnp.bfloat16)
        .reshape(tok_count, local_width)
    )
    return lax.psum_scatter(
        jnp.dot(normed, w_out, preferred_element_type=jnp.float32).astype(jnp.bfloat16),
        "tp",
        scatter_dimension=0,
        tiled=True,
    )


def solution(mesh):
    in_specs = (
        P("seq", "tp"),
        P("seq"),
        P(None, "tp"),
        P(None, "tp"),
        P(None, "tp"),
        P("tp"),
        P("tp", None),
    )
    out_specs = P(("seq", "tp"), None)
    return jax.shard_map(
        on_device, mesh=mesh, in_specs=in_specs, out_specs=out_specs, check_vma=False
    )
```

profile of v0, /device:TPU:1, one launch (start us, length us, event | category | flops | bytes accessed | tf_op | source)
XLA Modules:
  0.0 268.6 jit_solution(1697507522976406608)
XLA Ops:
  8.0 52.5 %all-gather.4.cloned.1.call-done = bf16[512,4096]{1,0:T(8,128)(2,1)} async-done(((bf16[512,1024]{1,0:T(8,128)(2,1)}), bf16[512,4096]{1,0:T(8,128)(2,1)}) %all-gather.4.cloned.1.call-update) | async-done | bytes 4194320 | tf_op jit(solution)/shard_map/all_gather | solution.py:30
  60.5 9.8 %fusion.6 = bf16[512,1024]{1,0:T(8,128)(2,1)S(1)} fusion(bf16[512,4096]{1,0:T(8,128)(2,1)} %all-gather.4.cloned.1.call-done, bf16[4096,1024]{1,0:T(8,128)(2,1)} %param.12, f32[512]{0:T(512)S(1)} %multiply_exponential_fusion), kind=kOutput, calls=%fused_computation.12 | convolution fusion | flops 4298113024 | bytes 13633536 | tf_op jit(solution)/shard_map/dot_general | solution.py:32
  70.9 9.1 %multiply_convert_fusion.2 = bf16[512,1024]{1,0:T(8,128)(2,1)S(1)} fusion(bf16[512,4096]{1,0:T(8,128)(2,1)} %all-gather.4.cloned.1.call-done, bf16[4096,1024]{1,0:T(8,128)(2,1)} %param.13, f32[512]{0:T(512)S(1)} %multiply_exponential_fusion), kind=kOutput, calls=%fused_computation.21 | convolution fusion | flops 4296015872 | bytes 13633536 | tf_op jit(solution)/shard_map/dot_general | solution.py:32
  80.6 1.2 fusion.25
  83.2 10.8 %fusion.14 = bf16[64,8,8,128]{3,2,1,0:T(8,128)(2,1)} fusion(bf16[512,4096]{1,0:T(8,128)(2,1)} %all-gather.4.cloned.1.call-done, bf16[4096,1024]{1,0:T(8,128)(2,1)} %param.11, f32[512]{0:T(512)S(1)} %multiply_exponential_fusion), kind=kOutput, calls=%fused_computation.23 | convolution fusion | flops 4298113024 | bytes 13633536 | tf_op jit(solution)/shard_map/dot_general | solution.py:32
  94.0 61.2 %all-gather.6.cloned.1.call-done = f32[256,128,128]{2,1,0:T(8,128)} async-done(((f32[8,128,128]{2,1,0:T(8,128)}), f32[256,128,128]{2,1,0:T(8,128)}) %all-gather.6.cloned.1.call-update) | async-done | bytes 16777232 | tf_op jit(solution)/shard_map/all_gather | solution.py:12
  155.1 40.0 %while.14 = (s32[]{:T(128)}, f32[8,128,128]{2,1,0:T(8,128)S(1)}, s32[]{:T(128)}, f32[32,8,128,128]{3,2,1,0:T(8,128)}, s32[]{:T(128)}, /*index=5*/s32[]{:T(128)}) while((s32[]{:T(128)}, f32[8,128,128]{2,1,0:T(8,128)S(1)}, s32[]{:T(128)}, f32[32,8,128,128]{3,2,1,0:T(8,128)}, s32[]{:T(128)}, /*index=5*/s32[]{:T(128)}) %tuple.42), condition=%wide.region_1.2_spmd.clone, body=%wide.region_0.1_spmd.clone.sunk | while | flops 393220 | bytes 1572965 | solution.py:20
  156.4 1.2 add_select_fusion.2
  157.6 1.2 add_select_fusion.2
  158.9 1.2 add_select_fusion.2
  160.1 1.2 add_select_fusion.2
  161.4 1.2 add_select_fusion.2
  162.6 1.2 add_select_fusion.2
  163.9 1.2 add_select_fusion.2
  165.2 1.2 add_select_fusion.2
  166.4 1.2 add_select_fusion.2
  167.7 1.2 add_select_fusion.2
  168.9 1.2 add_select_fusion.2
  170.2 1.2 add_select_fusion.2
  171.4 1.2 add_select_fusion.2
  172.7 1.2 add_select_fusion.2
  173.9 1.2 add_select_fusion.2
  175.2 1.2 add_select_fusion.2
  176.4 1.2 add_select_fusion.2
  177.7 1.2 add_select_fusion.2
  183.9 1.2 add_select_fusion.2
  193.9 1.2 add_select_fusion.2
  195.2 3.1 %fusion.17 = f32[8,128,512]{2,1,0:T(8,128)} fusion(bf16[64,8,8,128]{3,2,1,0:T(8,128)(2,1)} %fusion.14, f32[8,128,128]{2,1,0:T(8,128)S(1)} %get-tuple-element.84, f32[8,128,128]{2,1,0:T(8,128)S(1)} %copy-done), kind=kOutput, calls=%fused_computation.25 | convolution fusion | flops 134610944 | bytes 4194304 | tf_op jit(solution)/shard_map/bshd,bhde->bshe/dot_general | solution.py:52
  198.2 6.1 %fusion.10 = (f32[512,8]{0,1:T(8,128)S(1)}, f32[8,128,512]{2,1,0:T(8,128)}) fusion(f32[8,128,512]{2,1,0:T(8,128)} %fusion.17, bf16[512,8,128]{0,2,1:T(8,128)(2,1)S(1)} %bitcast.45, f32[512,512]{1,0:T(8,128)} %fusion.19, bf16[512,8,128]{0,2,1:T(8,128)(2,1)S(1)} %bitcast.43, bf16[64,8,8,128]{3,2,1,0:T(8,128)(2,1)} %fusion.14), kind=kOutput, calls=%fused_computation.18 | convolution fusion | flops 1079504896 | bytes 8404992 | tf_op jit(solution)/shard_map/bhst,bthe->bshe/dot_general | solution.py:56
  204.4 1.9 fusion.12
  206.3 9.5 %convolution_convert_fusion = bf16[512,4096]{1,0:T(8,128)(2,1)} fusion(bf16[512,1024]{0,1:T(8,128)(2,1)S(1)} %bitcast.46, bf16[1024,4096]{1,0:T(8,128)(2,1)} %param.15), kind=kOutput, calls=%fused_computation.6 | convolution fusion | flops 4297064448 | bytes 13631488 | tf_op jit(solution)/shard_map/dot_general | solution.py:66
  215.8 46.3 %reduce-scatter.2.cloned.1.call-done = bf16[128,4096]{1,0:T(8,128)(2,1)} async-done(((bf16[512,4096]{1,0:T(8,128)(2,1)}), bf16[128,4096]{1,0:T(8,128)(2,1)}) %reduce-scatter.2.cloned.1.call-update) | async-done | bytes 1048592 | tf_op jit(solution)/shard_map/reduce_scatter | solution.py:65
  (28 shorter events, 18.6 us)
Async XLA Ops:
  6.5 53.9 %all-gather.4.cloned.1.call-start = ((), (), s32[]{:S(2)}) async-start(), calls=%async_computation.1 | async-start | bytes 5242880 | tf_op jit(solution)/shard_map/all_gather | solution.py:30
  7.3 147.9 %all-gather.6.cloned.1.call-start = ((), (), s32[]{:S(2)}) async-start(), calls=%async_computation.3 | async-start | bytes 17301504 | tf_op jit(solution)/shard_map/all_gather | solution.py:12
  81.8 180.2 %reduce-scatter.2.cloned.1.call-start = ((), (), s32[]{:S(2)}) async-start(), calls=%async_computation.2 | async-start | bytes 5242880 | tf_op jit(solution)/shard_map/reduce_scatter | solution.py:65
  94.0 101.2 %copy-start = (f32[8,128,128]{2,1,0:T(8,128)S(1)}, f32[8,128,128]{2,1,0:T(8,128)}, u32[]{:S(2)}) copy-start(f32[8,128,128]{2,1,0:T(8,128)} %fusion.25) | copy-start | bytes 1572868
  198.2 6.1 %copy-start.1 = (f32[1024]{0:T(1024)S(1)}, f32[1024]{0:T(1024)}, u32[]{:S(2)}) copy-start(f32[1024]{0:T(1024)} %param.14) | copy-start | bytes 12292
Sparse Core Ops, SparseCore 0:
  9.0 51.4 all-gather.3
  82.0 73.1 all-gather.5
  215.9 46.0 reduce-scatter.1
where the time goes:
time: 270 us; the launch traced here: 269 us
  waiting for transfers between devices  161 us (60%)
  matrix products  49.7 us (18%)
  other arithmetic  42.9 us (16%)
  between operations  13.2 us (5%)
    all_gather x1, waiting for transfers between devices, prefix(): everything = lax.all_gather(x, axis)  61.2 us
    all_gather x1, waiting for transfers between devices, on_device(): piece = lax.all_gather(codes, 'tp', axis=1, tiled=True)  52.5 us
    reduce_scatter x1, waiting for transfers between devices, on_device(): lax.psum_scatter(jnp.dot(normed, w_out, preferred_element_type=jnp.float3...  46.3 us
    select_n x32, other arithmetic, step(): return jnp.where(reached, new, before)  39.3 us
    dot_general x3, matrix products, on_device(): jnp.dot(piece, weight, preferred_element_type=jnp.float32)  29.8 us
    dot_general x1, matrix products, on_device(): jnp.dot(normed, w_out, preferred_element_type=jnp.float32)  9.5 us
    dot_general x1, matrix products, on_device(): jnp.einsum('bhst,bthe->bshe', scores, value_b, preferred_element_type=jnp...  6.13 us
  transfers between devices with their start and end apart: 3, of which 3 were waited for; matrix products, arithmetic and copies ran while one was open for 5% of the time, Pallas kernels for 0%

commit v1 on v0

--- a/solution.py
+++ b/solution.py
@@ -5,6 +5,28 @@
 
 HD = 128
 BLK = 512
+
+
+def in_order(pieces, dim):
+    shape = list(pieces.shape[1:])
+    shape[dim] *= pieces.shape[0]
+    return jnp.moveaxis(pieces, 0, dim).reshape(shape)
+
+
+def collect(x, axis, dim):
+    peers = lax.axis_size(axis)
+    pairs = [(i, (i + 1) % peers) for i in range(peers)]
+    back = [(b, a) for a, b in pairs]
+    lower, upper = ([], [])
+    for hop in range(peers - 1):
+        if hop % 2 == 0:
+            lower.append(lax.ppermute(lower[-1] if lower else x, axis, pairs))
+        else:
+            upper.append(lax.ppermute(upper[-1] if upper else x, axis, back))
+    tiles = jnp.stack([*lower[::-1], x, *upper])
+    shift = lax.axis_index(axis) - len(lower)
+    tiles = tiles[(jnp.arange(peers) - shift) % peers]
+    return in_order(tiles, dim)
 
 
 def prefix(x, axis, combine, identity):
@@ -27,7 +49,7 @@
     blocks = tok_count // BLK
     row_scale = jnp.exp2(exponents.astype(jnp.float32))[:, None]
     weights = (w_query, w_key, w_value)
-    piece = lax.all_gather(codes, "tp", axis=1, tiled=True)
+    piece = collect(codes, "tp", 1)
     query, keys, values = tuple(
         (jnp.dot(piece, weight, preferred_element_type=jnp.float32) for weight in weights)
     )

time: 270 us -> 280 us (1.037)
  local copies, waits for them, and re-layouts: 1.09 us -> 12.7 us
  waiting for transfers between devices: 161 us -> 155 us
  starting transfers between devices: 0.26 us -> 4.8 us
  matrix products: 49.7 us -> 46.7 us
    all_gather x1 -> x0, waiting for transfers between devices: 52.5 us -> none  [on_device(): piece = lax.all_gather(codes, 'tp', axis=1, tiled=True)]
    ppermute x0 -> x3, waiting for transfers between devices: none -> 47 us  [the longest x2 47 us: collect(): lower.append(lax.ppermute(lower[-1] if lower else x, axis, pairs))]
    transpose x0 -> x1, local copies, waits for them, and re-layouts: none -> 6.2 us  [in_order(): return jnp.moveaxis(pieces, 0, dim).reshape(shape)]
    gather x0 -> x1, local copies, waits for them, and re-layouts: none -> 4.95 us  [collect(): tiles = tiles[(jnp.arange(peers) - shift) % peers]]
    ppermute x0 -> x3, starting transfers between devices: none -> 4.58 us  [the longest x2 2.46 us: collect(): lower.append(lax.ppermute(lower[-1] if lower else x, axis, pairs))]
    another operation x0 -> x1, other arithmetic: none -> 3.28 us  [collect(): tiles = jnp.stack([*lower[::-1], x, *upper])]
  transfers between devices with their start and end apart: 3 -> 5, of which waited for: 3 -> 4; matrix products, arithmetic and copies ran while one was open for 5% -> 4% of each run, Pallas kernels for 0% -> 0%
where the time goes in v1:
time: 280 us; the launch traced here: 279 us
  waiting for transfers between devices  155 us (55%)
  matrix products  46.7 us (17%)
  other arithmetic  44.6 us (16%)
  between operations  13.5 us (5%)
  local copies, waits for them, and re-layouts  12.7 us (5%)
  starting transfers between devices  4.8 us (2%)
    all_gather x1, waiting for transfers between devices, prefix(): everything = lax.all_gather(x, axis)  62.1 us
    ppermute x2, waiting for transfers between devices, collect(): lower.append(lax.ppermute(lower[-1] if lower else x, axis, pairs))  47 us
    reduce_scatter x1, waiting for transfers between devices, on_device(): lax.psum_scatter(jnp.dot(normed, w_out, preferred_element_type=jnp.float3...  46.3 us
    select_n x32, other arithmetic, step(): return jnp.where(reached, new, before)  39.3 us
    dot_general x3, matrix products, on_device(): jnp.dot(piece, weight, preferred_element_type=jnp.float32)  28.9 us
    dot_general x1, matrix products, on_device(): jnp.dot(normed, w_out, preferred_element_type=jnp.float32)  9.51 us
    transpose x1, local copies, waits for them, and re-layouts, in_order(): return jnp.moveaxis(pieces, 0, dim).reshape(shape)  6.2 us
  transfers between devices with their start and end apart: 5, of which 4 were waited for; matrix products, arithmetic and copies ran while one was open for 4% of the time, Pallas kernels for 0%

profile of v1, /device:TPU:1, one launch (start us, length us, event | category | flops | bytes accessed | tf_op | source)
XLA Modules:
  0.0 278.5 jit_solution(12882523355125753035)
XLA Ops:
  6.5 2.5 collective-permute-start
  9.0 2.1 collective-permute-start.2
  11.1 23.1 %collective-permute-done = bf16[512,1024]{1,0:T(8,128)(2,1)S(1)} collective-permute-done((bf16[512,1024]{1,0:T(8,128)(2,1)}, bf16[512,1024]{1,0:T(8,128)(2,1)S(1)}, u32[]{:S(2)}, u32[]{:S(2)}) %collective-permute-start) | collective-permute-done | bytes 1048608 | tf_op jit(solution)/shard_map/ppermute | solution.py:23
  34.9 24.0 %collective-permute-done.1 = bf16[512,1024]{1,0:T(8,128)(2,1)S(1)} collective-permute-done((bf16[512,1024]{1,0:T(8,128)(2,1)S(1)}, bf16[512,1024]{1,0:T(8,128)(2,1)S(1)}, u32[]{:S(2)}, u32[]{:S(2)}) %collective-permute-start.1) | collective-permute-done | bytes 1048608 | tf_op jit(solution)/shard_map/ppermute | solution.py:23
  58.9 3.3 %pad_maximum_fusion = bf16[4,512,1024]{2,1,0:T(8,128)(2,1)} fusion(bf16[1,512,1024]{2,1,0:T(8,128)(2,1)S(1)} %bitcast.66, bf16[1,512,1024]{2,1,0:T(8,128)(2,1)} %bitcast.64, bf16[1,512,1024]{2,1,0:T(8,128)(2,1)S(1)} %bitcast.65, bf16[1,512,1024]{2,1,0:T(8,128)(2,1)S(1)} %bitcast.67), kind=kLoop, calls=%fused_computation.9 | loop fusion | flops 6291456 | bytes 8388608 | tf_op jit(solution)/shard_map/stack | solution.py:26
  62.1 4.9 %gather_fusion = bf16[4,512,1024]{2,1,0:T(8,128)(2,1)} fusion(bf16[4,512,1024]{2,1,0:T(8,128)(2,1)} %pad_maximum_fusion, s32[1024]{0:T(1024)S(1)} %pad_clamp_fusion), kind=kCustom, calls=%fused_computation | custom fusion | bytes 8388624 | tf_op jit(solution)/shard_map/gather | solution.py:28
  67.1 6.2 %copy.26 = bf16[512,4,1024]{0,2,1:T(8,128)(2,1)} copy(bf16[512,4,1024]{2,0,1:T(8,128)(2,1)} %bitcast.57) | data formatting | bytes 8388608 | tf_op jit(solution)/shard_map/transpose | solution.py:13
  73.3 9.2 %multiply_convert_fusion.2 = bf16[512,1024]{1,0:T(8,128)(2,1)S(1)} fusion(bf16[512,4096]{0,1:T(8,128)(2,1)} %bitcast.58, bf16[4096,1024]{1,0:T(8,128)(2,1)} %param.13, f32[512]{0:T(512)S(1)} %multiply_exponential_fusion), kind=kOutput, calls=%fused_computation.23 | convolution fusion | flops 4296015872 | bytes 13633536 | tf_op jit(solution)/shard_map/dot_general | solution.py:54
  83.0 9.9 %fusion.15 = bf16[64,8,8,128]{3,2,1,0:T(8,128)(2,1)S(1)} fusion(bf16[512,4096]{0,1:T(8,128)(2,1)} %bitcast.59, bf16[4096,1024]{1,0:T(8,128)(2,1)} %param.12, f32[512]{0:T(512)S(1)} %multiply_exponential_fusion), kind=kOutput, calls=%fused_computation.26 | convolution fusion | flops 4298113024 | bytes 13633536 | tf_op jit(solution)/shard_map/dot_general | solution.py:54
  93.8 1.3 fusion.20
  96.5 9.9 %fusion.14 = bf16[64,8,8,128]{3,2,1,0:T(8,128)(2,1)S(1)} fusion(bf16[512,4096]{0,1:T(8,128)(2,1)} %bitcast.60, bf16[4096,1024]{1,0:T(8,128)(2,1)} %param.11, f32[512]{0:T(512)S(1)} %multiply_exponential_fusion), kind=kOutput, calls=%fused_computation.25 | convolution fusion | flops 4298113024 | bytes 13633536 | tf_op jit(solution)/shard_map/dot_general | solution.py:54
  106.4 62.1 %all-gather.3.cloned.1.call-done = f32[256,128,128]{2,1,0:T(8,128)} async-done(((f32[8,128,128]{2,1,0:T(8,128)}), f32[256,128,128]{2,1,0:T(8,128)}) %all-gather.3.cloned.1.call-update) | async-done | bytes 16777232 | tf_op jit(solution)/shard_map/all_gather | solution.py:34
  168.5 40.0 %while.14 = (s32[]{:T(128)}, f32[8,128,128]{2,1,0:T(8,128)S(1)}, s32[]{:T(128)}, f32[32,8,128,128]{3,2,1,0:T(8,128)}, s32[]{:T(128)}, /*index=5*/s32[]{:T(128)}) while((s32[]{:T(128)}, f32[8,128,128]{2,1,0:T(8,128)S(1)}, s32[]{:T(128)}, f32[32,8,128,128]{3,2,1,0:T(8,128)}, s32[]{:T(128)}, /*index=5*/s32[]{:T(128)}) %tuple.40), condition=%wide.region_1.2_spmd.clone, body=%wide.region_0.1_spmd.clone.sunk | while | flops 393220 | bytes 1572965 | solution.py:42
  169.8 1.2 add_select_fusion.2
  171.0 1.2 add_select_fusion.2
  172.3 1.2 add_select_fusion.2
  173.5 1.2 add_select_fusion.2
  174.8 1.2 add_select_fusion.2
  176.0 1.2 add_select_fusion.2
  177.3 1.2 add_select_fusion.2
  178.5 1.2 add_select_fusion.2
  179.8 1.2 add_select_fusion.2
  181.0 1.2 add_select_fusion.2
  182.3 1.2 add_select_fusion.2
  183.5 1.2 add_select_fusion.2
  184.8 1.2 add_select_fusion.2
  186.0 1.2 add_select_fusion.2
  199.8 1.2 add_select_fusion.2
  208.6 1.8 fusion.18
  210.4 5.1 %fusion.10 = (f32[512,8]{0,1:T(8,128)S(1)}, f32[8,128,512]{2,1,0:T(8,128)S(1)}) fusion(f32[8,128,512]{2,1,0:T(8,128)} %fusion.18, bf16[512,8,128]{0,2,1:T(8,128)(2,1)S(1)} %bitcast.62, f32[512,512]{1,0:T(8,128)} %fusion.24, bf16[64,8,8,128]{3,2,1,0:T(8,128)(2,1)} %copy-done.2, bf16[64,8,8,128]{3,2,1,0:T(8,128)(2,1)} %copy-done.1), kind=kOutput, calls=%fused_computation.20 | convolution fusion | flops 1079504896 | bytes 8404992 | tf_op jit(solution)/shard_map/bhst,bthe->bshe/dot_general | solution.py:78
  215.9 9.5 %convolution_convert_fusion = bf16[512,4096]{1,0:T(8,128)(2,1)} fusion(bf16[512,1024]{0,1:T(8,128)(2,1)S(1)} %bitcast.63, bf16[1024,4096]{1,0:T(8,128)(2,1)} %param.15), kind=kOutput, calls=%fused_computation.7 | convolution fusion | flops 4297064448 | bytes 13631488 | tf_op jit(solution)/shard_map/dot_general | solution.py:88
  225.4 46.3 %reduce-scatter.2.cloned.1.call-done = bf16[128,4096]{1,0:T(8,128)(2,1)} async-done(((bf16[512,4096]{1,0:T(8,128)(2,1)}), bf16[128,4096]{1,0:T(8,128)(2,1)}) %reduce-scatter.2.cloned.1.call-update) | async-done | bytes 1048592 | tf_op jit(solution)/shard_map/reduce_scatter | solution.py:87
  (39 shorter events, 24.7 us)
Async XLA Ops:
  6.5 162.0 %all-gather.3.cloned.1.call-start = ((), (), s32[]{:S(2)}) async-start(), calls=%async_computation.2 | async-start | bytes 17301504 | tf_op jit(solution)/shard_map/all_gather | solution.py:34
  6.5 27.6 %collective-permute-start = (bf16[512,1024]{1,0:T(8,128)(2,1)}, bf16[512,1024]{1,0:T(8,128)(2,1)S(1)}, u32[]{:S(2)}, u32[]{:S(2)}) collective-permute-start(bf16[512,1024]{1,0:T(8,128)(2,1)} %param.9), channel_id=1, source_target_pairs={{0,1},{1,2},{2,3},{3,0},{4,5},{5,6},{6,7},{7,4},{8,9},{9,10},{10,1... | collective-permute-start | bytes 3145736 | tf_op jit(solution)/shard_map/ppermute | solution.py:23
  9.0 25.9 %collective-permute-start.2 = (bf16[512,1024]{1,0:T(8,128)(2,1)}, bf16[512,1024]{1,0:T(8,128)(2,1)S(1)}, u32[]{:S(2)}, u32[]{:S(2)}) collective-permute-start(bf16[512,1024]{1,0:T(8,128)(2,1)} %param.9), channel_id=1, source_target_pairs={{1,0},{2,1},{3,2},{0,3},{5,4},{6,5},{7,6},{4,7},{9,8},{10,9},{11,1... | collective-permute-start | bytes 3145736 | tf_op jit(solution)/shard_map/ppermute | solution.py:25
  34.2 24.7 %collective-permute-start.1 = (bf16[512,1024]{1,0:T(8,128)(2,1)S(1)}, bf16[512,1024]{1,0:T(8,128)(2,1)S(1)}, u32[]{:S(2)}, u32[]{:S(2)}) collective-permute-start(bf16[512,1024]{1,0:T(8,128)(2,1)S(1)} %collective-permute-done), channel_id=1, source_target_pairs={{0,1},{1,2},{2,3},{3,0},{4,5},{5,6},{6,7},{7,4},{8,9},{9,10},{10,1... | collective-permute-start | bytes 3145736 | tf_op jit(solution)/shard_map/ppermute | solution.py:23
  92.9 1.0 copy-start.1
  95.2 176.5 %reduce-scatter.2.cloned.1.call-start = ((), (), s32[]{:S(2)}) async-start(), calls=%async_computation.1 | async-start | bytes 5242880 | tf_op jit(solution)/shard_map/reduce_scatter | solution.py:87
  106.4 102.1 %copy-start.2 = (bf16[64,8,8,128]{3,2,1,0:T(8,128)(2,1)}, bf16[64,8,8,128]{3,2,1,0:T(8,128)(2,1)S(1)}, u32[]{:S(2)}) copy-start(bf16[64,8,8,128]{3,2,1,0:T(8,128)(2,1)S(1)} %fusion.14) | copy-start | bytes 3145732
  106.4 102.1 %copy-start = (f32[8,128,128]{2,1,0:T(8,128)S(1)}, f32[8,128,128]{2,1,0:T(8,128)}, u32[]{:S(2)}) copy-start(f32[8,128,128]{2,1,0:T(8,128)} %fusion.20) | copy-start | bytes 1572868
  210.4 5.2 %copy-start.3 = (f32[1024]{0:T(1024)S(1)}, f32[1024]{0:T(1024)}, u32[]{:S(2)}) copy-start(f32[1024]{0:T(1024)} %param.14) | copy-start | bytes 12292
Sparse Core Ops, SparseCore 0:
  95.3 73.1 all-gather.2
  225.5 46.1 reduce-scatter.1
